TPU v7x, 32 devices: a whole 2x2x4 slice. The times are simulated.
32 devices in a mesh: dp: 16 (over z, x, core), tensor: 2 (over y).
Axes of the slice: x: 2, y: 2, z: 4, core: 2. Of those that a mesh axis runs over, the one named last changes fastest.
Arguments:
- features: bfloat16 [512, 16, 4096], P('tensor', 'dp'), may hold values from -6 to 6
- cotangent: bfloat16 [512, 16, 4096], P('tensor', 'dp'), may hold values from -6 to 6
- embedding: bfloat16 [16, 2048], P('dp'), may hold values from -6 to 6
- context: bfloat16 [16, 260, 2048], P('dp'), may hold values from -6 to 6
- lengths: int32 [16], P('dp'), may hold values from 5 to 256, as said below
- norm1_gain: float32 [512], P('tensor'), may hold values from 0.25 to 1.75
- norm1_bias: float32 [512], P('tensor'), may hold values from -2 to 2
- conv1_weight: bfloat16 [512, 4608], P('tensor'), may hold values from -0.09375 to 0.09375
- conv1_bias: float32 [512], P('tensor'), may hold values from -2 to 2
- emb_weight: bfloat16 [2, 2048, 512], P(None, None, 'tensor'), may hold values from -0.125 to 0.125
- emb_bias: float32 [2, 512], P(None, 'tensor'), may hold values from -2 to 2
- norm2_gain: float32 [512], P('tensor'), may hold values from 0.25 to 1.75
- norm2_bias: float32 [512], P('tensor'), may hold values from -2 to 2
- conv2_weight: bfloat16 [512, 4608], P('tensor'), may hold values from -0.09375 to 0.09375
- conv2_bias: float32 [512], P('tensor'), may hold values from -2 to 2
- norm3_gain: float32 [512], P('tensor'), may hold values from 0.25 to 1.75
- norm3_bias: float32 [512], P('tensor'), may hold values from -2 to 2
- qkv_weight: bfloat16 [3, 512, 512], P(None, 'tensor'), may hold values from -0.25 to 0.25
- qkv_bias: float32 [3, 512], P(None, 'tensor'), may hold values from -2 to 2
- context_weight: bfloat16 [2, 512, 2048], P(None, 'tensor'), may hold values from -0.125 to 0.125
- context_bias: float32 [2, 512], P(None, 'tensor'), may hold values from -2 to 2
- out_weight: bfloat16 [512, 512], P('tensor'), may hold values from -2 to 2
- out_bias: float32 [512], P('tensor'), may hold values from -2 to 2
Outputs:
- output: bfloat16 [512, 16, 4096], P('tensor', 'dp')
- input_grad: float32 [512, 16, 4096], P('tensor', 'dp')
- norm1_gain_grad: float32 [512], P('tensor')
- norm1_bias_grad: float32 [512], P('tensor')
- conv1_weight_grad: float32 [512, 4608], P('tensor')
- conv1_bias_grad: float32 [512], P('tensor')
- emb_weight_grad: float32 [2, 2048, 512], P(None, None, 'tensor')
- emb_bias_grad: float32 [2, 512], P(None, 'tensor')
- norm2_gain_grad: float32 [512], P('tensor')
- norm2_bias_grad: float32 [512], P('tensor')
- conv2_weight_grad: float32 [512, 4608], P('tensor')
- conv2_bias_grad: float32 [512], P('tensor')
- norm3_gain_grad: float32 [512], P('tensor')
- norm3_bias_grad: float32 [512], P('tensor')
- qkv_weight_grad: float32 [3, 512, 512], P(None, 'tensor')
- qkv_bias_grad: float32 [3, 512], P(None, 'tensor')
- context_weight_grad: float32 [2, 512, 2048], P(None, 'tensor')
- context_bias_grad: float32 [2, 512], P(None, 'tensor')
- out_weight_grad: float32 [512, 512], P('tensor')
- out_bias_grad: float32 [512], P('tensor')
Inputs may be any that keep to these rules, and one draw needn't show every extreme that they name: `lengths`: each image's number of real text tokens; some image has 256.
All inputs are finite; a program needn't handle non-finite values.
Results may differ from a plain program's by a relative error of at most 0.025.
Values may be sent and summed in bfloat16 or wider, within the bound.
No kernel may reach another device: no remote copies, remote signals or barrier semaphores. Data moves between devices by JAX's collectives and lax.ppermute only.
A program may use at most 384 MiB of HBM per device.

v0:
```python
import jax
import jax.numpy as jnp
from jax import lax
from jax.sharding import PartitionSpec as P

C = 512
HEAD_DIM = 64
GROUPS = 32
SIDE = 64
HW = 4096
CTX = 260
EPSILON = 1e-05
NEG_FILL = -1e30


def group_norm(values, gain_vec, bias_vec):
    channels, images, pixels = values.shape
    per_group = C // GROUPS
    grouped = values.reshape(channels // per_group, per_group, images, pixels)
    group_mean = jnp.mean(grouped, axis=(1, 3), keepdims=True)
    group_var = jnp.mean(jnp.square(grouped - group_mean), axis=(1, 3), keepdims=True)
    normal_vals = ((grouped - group_mean) * lax.rsqrt(group_var + EPSILON)).reshape(values.shape)
    return normal_vals * gain_vec[:, None, None] + bias_vec[:, None, None]


def shifted(values, kernel_tap):
    row_off, col_off = (kernel_tap // 3, kernel_tap % 3)
    channels, images, pixels = values.shape
    padded = jnp.pad(values.reshape(channels, images, SIDE, SIDE), ((0, 0), (0, 0), (1, 1), (1, 1)))
    return padded[:, :, row_off : row_off + SIDE, col_off : col_off + SIDE].reshape(
        channels, images, pixels
    )


def convolve(full_act, weight, bias_vec):
    kernel = weight.reshape(weight.shape[0], 9, C)
    result = (
        jnp.zeros((weight.shape[0],) + full_act.shape[1:], jnp.float32) + bias_vec[:, None, None]
    )
    for kernel_tap in range(9):
        result = result + jnp.einsum(
            "oc,cip->oip",
            kernel[:, kernel_tap],
            shifted(full_act, kernel_tap),
            preferred_element_type=jnp.float32,
        )
    return result


def kernel_grad(grad_low, full_act):
    pieces = [
        jnp.einsum(
            "oip,cip->oc",
            grad_low,
            shifted(full_act, kernel_tap),
            preferred_element_type=jnp.float32,
        )
        for kernel_tap in range(9)
    ]
    return jnp.stack(pieces, axis=1).reshape(grad_low.shape[0], 9 * C)


def conv_input_grad(grad_low, weight):
    channels = grad_low.shape[0]
    kernel = weight.reshape(channels, 9, C)
    moved_grads = [shifted(grad_low, 8 - kernel_tap) for kernel_tap in range(9)]
    result = jnp.zeros((lax.axis_size("tensor") * channels,) + grad_low.shape[1:], jnp.float32)
    for kernel_tap in range(9):
        cols_part = kernel[:, kernel_tap]
        result = result + jnp.einsum(
            "oc,oip->cip", cols_part, moved_grads[kernel_tap], preferred_element_type=jnp.float32
        )
    return lax.psum_scatter(
        result.astype(jnp.bfloat16), "tensor", scatter_dimension=0, tiled=True
    ).astype(jnp.float32)


def to_heads(values):
    channels, images, length_n = values.shape
    return (
        values.reshape(channels // HEAD_DIM, HEAD_DIM, images, length_n)
        .transpose(2, 0, 1, 3)
        .reshape(-1, HEAD_DIM, length_n)
    )


def from_heads(values, images):
    groups_n, head_dims, length_n = values.shape
    heads_here = groups_n // images
    return (
        values.reshape(images, heads_here, head_dims, length_n)
        .transpose(1, 2, 0, 3)
        .reshape(heads_here * head_dims, images, length_n)
    )


def masked_scores(q_block, key_rows, key_valid):
    scores = jnp.einsum(
        "gdi,gdj->gij", q_block, key_rows, preferred_element_type=jnp.float32
    ) * HEAD_DIM ** (-0.5)
    return jnp.where(key_valid[:, None, :], scores, NEG_FILL)


def attend_forward(queries, key_rows, value_rows, key_valid):
    groups_n = queries.shape[0]
    block_len = min(512, HW)
    blocks_q = queries.reshape(groups_n, HEAD_DIM, HW // block_len, block_len).transpose(2, 0, 1, 3)

    def one_block(q_block):
        scores = masked_scores(q_block, key_rows, key_valid)
        row_top = jnp.max(scores, axis=-1, keepdims=True)
        raised = jnp.exp(scores - row_top)
        row_total = jnp.sum(raised, axis=-1, keepdims=True)
        probs_low = (raised / row_total).astype(jnp.bfloat16)
        mixed_out = jnp.einsum(
            "gdj,gij->gdi", value_rows, probs_low, preferred_element_type=jnp.float32
        )
        return (mixed_out.astype(jnp.bfloat16), row_top, row_total)

    mixed_out, row_top, row_total = lax.map(one_block, blocks_q)
    merged = mixed_out.transpose(1, 2, 0, 3).reshape(groups_n, HEAD_DIM, HW)
    return (merged, row_top, row_total)


def attend_backward(queries, key_rows, value_rows, key_valid, grad_mixed, row_top, row_total):
    groups_n = queries.shape[0]
    block_len = min(512, HW)
    count_b = HW // block_len
    blocks_q = queries.reshape(groups_n, HEAD_DIM, count_b, block_len).transpose(2, 0, 1, 3)
    blocks_g = grad_mixed.reshape(groups_n, HEAD_DIM, count_b, block_len).transpose(2, 0, 1, 3)
    scale_val = HEAD_DIM ** (-0.5)

    def one_block(carried, packed):
        key_acc, value_acc = carried
        q_block, g_block, block_top, block_total = packed
        scores = masked_scores(q_block, key_rows, key_valid)
        prob_f32 = jnp.exp(scores - block_top) / block_total
        probs_low = prob_f32.astype(jnp.bfloat16)
        value_acc = value_acc + jnp.einsum(
            "gdi,gij->gdj", g_block, probs_low, preferred_element_type=jnp.float32
        )
        grad_probs = jnp.einsum(
            "gdi,gdj->gij", g_block, value_rows, preferred_element_type=jnp.float32
        )
        delta_row = jnp.sum(prob_f32 * grad_probs, axis=-1, keepdims=True)
        grad_scores = (prob_f32 * (grad_probs - delta_row)).astype(jnp.bfloat16)
        grad_query = (
            jnp.einsum("gij,gdj->gdi", grad_scores, key_rows, preferred_element_type=jnp.float32)
            * scale_val
        )
        key_acc = (
            key_acc
            + jnp.einsum("gij,gdi->gdj", grad_scores, q_block, preferred_element_type=jnp.float32)
            * scale_val
        )
        return ((key_acc, value_acc), grad_query)

    zero_acc = jnp.zeros(key_rows.shape, jnp.float32)
    (key_grad, value_grad), query_grad = lax.scan(
        one_block, (zero_acc, zero_acc), (blocks_q, blocks_g, row_top, row_total)
    )
    query_grad = query_grad.transpose(1, 2, 0, 3).reshape(groups_n, HEAD_DIM, HW)
    return (query_grad, key_grad, value_grad)


def first_section(values, gain_vec, bias_vec):
    return jax.nn.silu(group_norm(values, gain_vec, bias_vec))


def second_section(values, gain_vec, bias_vec, modulation):
    normal_vals = group_norm(values, gain_vec, bias_vec)
    return jax.nn.silu(normal_vals * (1.0 + modulation[0][:, :, None]) + modulation[1][:, :, None])


def local(
    features,
    cotangent,
    embedding,
    context,
    lengths,
    norm1_gain,
    norm1_bias,
    conv1_weight,
    conv1_bias,
    emb_weight,
    emb_bias,
    norm2_gain,
    norm2_bias,
    conv2_weight,
    conv2_bias,
    norm3_gain,
    norm3_bias,
    qkv_weight,
    qkv_bias,
    context_weight,
    context_bias,
    out_weight,
    out_bias,
):
    channels, images, pixels = features.shape
    feat_f32 = features.astype(jnp.float32)
    act_one = first_section(feat_f32, norm1_gain, norm1_bias).astype(jnp.bfloat16)
    full_one = lax.all_gather(act_one, "tensor", axis=0, tiled=True)
    conv_one = convolve(full_one, conv1_weight, conv1_bias)
    emb_act = jax.nn.silu(embedding.astype(jnp.float32)).astype(jnp.bfloat16)
    scale_shift = (
        jnp.einsum("ie,teo->toi", emb_act, emb_weight, preferred_element_type=jnp.float32)
        + emb_bias[:, :, None]
    )
    act_two = second_section(conv_one, norm2_gain, norm2_bias, scale_shift).astype(jnp.bfloat16)
    full_two = lax.all_gather(act_two, "tensor", axis=0, tiled=True)
    hidden = feat_f32 + convolve(full_two, conv2_weight, conv2_bias)
    normed = group_norm(hidden, norm3_gain, norm3_bias).astype(jnp.bfloat16)
    full_three = lax.all_gather(normed, "tensor", axis=0, tiled=True)
    qkv_low = (
        jnp.einsum("toc,cip->toip", qkv_weight, full_three, preferred_element_type=jnp.float32)
        + qkv_bias[:, :, None, None]
    ).astype(jnp.bfloat16)
    ctx_low = (
        jnp.einsum("toe,ine->toin", context_weight, context, preferred_element_type=jnp.float32)
        + context_bias[:, :, None, None]
    ).astype(jnp.bfloat16)
    queries = to_heads(qkv_low[0])
    key_rows = jnp.concatenate([to_heads(qkv_low[1]), to_heads(ctx_low[0])], axis=2)
    value_rows = jnp.concatenate([to_heads(qkv_low[2]), to_heads(ctx_low[1])], axis=2)
    key_limit = HW + 4 + lengths
    key_valid = jnp.repeat(
        jnp.arange(HW + CTX, dtype=jnp.int32)[None, :] < key_limit[:, None],
        channels // HEAD_DIM,
        axis=0,
    )
    heads_mixed, row_top, row_total = attend_forward(queries, key_rows, value_rows, key_valid)
    heads_out = from_heads(heads_mixed, images)
    full_heads = lax.all_gather(heads_out, "tensor", axis=0, tiled=True)
    output = (
        hidden
        + jnp.einsum("oc,cip->oip", out_weight, full_heads, preferred_element_type=jnp.float32)
        + out_bias[:, None, None]
    ).astype(jnp.bfloat16)
    grad_top = cotangent.astype(jnp.float32)
    out_weight_grad = jnp.einsum(
        "oip,cip->oc", cotangent, full_heads, preferred_element_type=jnp.float32
    )
    out_bias_grad = jnp.sum(grad_top, axis=(1, 2))
    cols_part = out_weight
    grad_heads = lax.psum_scatter(
        jnp.einsum("oc,oip->cip", cols_part, cotangent, preferred_element_type=jnp.float32).astype(
            jnp.bfloat16
        ),
        "tensor",
        scatter_dimension=0,
        tiled=True,
    )
    query_grad, key_grad, value_grad = attend_backward(
        queries, key_rows, value_rows, key_valid, to_heads(grad_heads), row_top, row_total
    )
    grad_qkv = jnp.stack(
        [
            from_heads(query_grad, images),
            from_heads(key_grad[:, :, :HW], images),
            from_heads(value_grad[:, :, :HW], images),
        ]
    ).astype(jnp.bfloat16)
    grad_ctx = jnp.stack(
        [from_heads(key_grad[:, :, HW:], images), from_heads(value_grad[:, :, HW:], images)]
    ).astype(jnp.bfloat16)
    qkv_weight_grad = jnp.einsum(
        "toip,cip->toc", grad_qkv, full_three, preferred_element_type=jnp.float32
    )
    qkv_bias_grad = jnp.sum(grad_qkv.astype(jnp.float32), axis=(2, 3))
    context_weight_grad = jnp.einsum(
        "toin,ine->toe", grad_ctx, context, preferred_element_type=jnp.float32
    )
    context_bias_grad = jnp.sum(grad_ctx.astype(jnp.float32), axis=(2, 3))
    cols_part = qkv_weight
    grad_normed = lax.psum_scatter(
        jnp.einsum("toc,toip->cip", cols_part, grad_qkv, preferred_element_type=jnp.float32).astype(
            jnp.bfloat16
        ),
        "tensor",
        scatter_dimension=0,
        tiled=True,
    ).astype(jnp.float32)
    unused_three, pull_three = jax.vjp(group_norm, hidden, norm3_gain, norm3_bias)
    grad_branch, norm3_gain_grad, norm3_bias_grad = pull_three(grad_normed)
    grad_hidden = grad_top + grad_branch
    attention_grads = (
        lax.psum(out_weight_grad.astype(jnp.bfloat16), "dp").astype(jnp.float32),
        lax.psum(out_bias_grad.astype(jnp.bfloat16), "dp").astype(jnp.float32),
        lax.psum(qkv_weight_grad.astype(jnp.bfloat16), "dp").astype(jnp.float32),
        lax.psum(qkv_bias_grad.astype(jnp.bfloat16), "dp").astype(jnp.float32),
        lax.psum(context_weight_grad.astype(jnp.bfloat16), "dp").astype(jnp.float32),
        lax.psum(context_bias_grad.astype(jnp.bfloat16), "dp").astype(jnp.float32),
        lax.psum(norm3_gain_grad.astype(jnp.bfloat16), "dp").astype(jnp.float32),
        lax.psum(norm3_bias_grad.astype(jnp.bfloat16), "dp").astype(jnp.float32),
    )
    grad_conv_two = grad_hidden.astype(jnp.bfloat16)
    conv2_bias_grad = jnp.sum(grad_conv_two.astype(jnp.float32), axis=(1, 2))
    conv2_weight_grad = kernel_grad(grad_conv_two, full_two)
    grad_act_two = conv_input_grad(grad_conv_two, conv2_weight)
    unused_two, pull_two = jax.vjp(second_section, conv_one, norm2_gain, norm2_bias, scale_shift)
    grad_conv_one, norm2_gain_grad, norm2_bias_grad, grad_modulation = pull_two(grad_act_two)
    grad_mod_low = grad_modulation.astype(jnp.bfloat16)
    emb_weight_grad = jnp.einsum(
        "ie,toi->teo", emb_act, grad_mod_low, preferred_element_type=jnp.float32
    )
    emb_bias_grad = jnp.sum(grad_mod_low.astype(jnp.float32), axis=2)
    grad_conv_low = grad_conv_one.astype(jnp.bfloat16)
    conv1_bias_grad = jnp.sum(grad_conv_low.astype(jnp.float32), axis=(1, 2))
    conv1_weight_grad = kernel_grad(grad_conv_low, full_one)
    grad_act_one = conv_input_grad(grad_conv_low, conv1_weight)
    unused_one, pull_one = jax.vjp(first_section, feat_f32, norm1_gain, norm1_bias)
    grad_feat, norm1_gain_grad, norm1_bias_grad = pull_one(grad_act_one)
    input_grad = grad_hidden + grad_feat
    residual_grads = (
        lax.psum(norm1_gain_grad.astype(jnp.bfloat16), "dp").astype(jnp.float32),
        lax.psum(norm1_bias_grad.astype(jnp.bfloat16), "dp").astype(jnp.float32),
        lax.psum(conv1_weight_grad.astype(jnp.bfloat16), "dp").astype(jnp.float32),
        lax.psum(conv1_bias_grad.astype(jnp.bfloat16), "dp").astype(jnp.float32),
        lax.psum(emb_weight_grad.astype(jnp.bfloat16), "dp").astype(jnp.float32),
        lax.psum(emb_bias_grad.astype(jnp.bfloat16), "dp").astype(jnp.float32),
        lax.psum(norm2_gain_grad.astype(jnp.bfloat16), "dp").astype(jnp.float32),
        lax.psum(norm2_bias_grad.astype(jnp.bfloat16), "dp").astype(jnp.float32),
        lax.psum(conv2_weight_grad.astype(jnp.bfloat16), "dp").astype(jnp.float32),
        lax.psum(conv2_bias_grad.astype(jnp.bfloat16), "dp").astype(jnp.float32),
    )
    return (
        output,
        input_grad,
        residual_grads[0],
        residual_grads[1],
        residual_grads[2],
        residual_grads[3],
        residual_grads[4],
        residual_grads[5],
        residual_grads[6],
        residual_grads[7],
        residual_grads[8],
        residual_grads[9],
        attention_grads[6],
        attention_grads[7],
        attention_grads[2],
        attention_grads[3],
        attention_grads[4],
        attention_grads[5],
        attention_grads[0],
        attention_grads[1],
    )


def solution(mesh):
    placed = (
        P("tensor", "dp", None),
        P("tensor", "dp", None),
        P("dp", None),
        P("dp", None, None),
        P("dp"),
        P("tensor"),
        P("tensor"),
        P("tensor", None),
        P("tensor"),
        P(None, None, "tensor"),
        P(None, "tensor"),
        P("tensor"),
        P("tensor"),
        P("tensor", None),
        P("tensor"),
        P("tensor"),
        P("tensor"),
        P(None, "tensor", None),
        P(None, "tensor"),
        P(None, "tensor", None),
        P(None, "tensor"),
        P("tensor", None),
        P("tensor"),
    )
    return jax.shard_map(
        local,
        mesh=mesh,
        in_specs=placed,
        out_specs=(
            P("tensor", "dp", None),
            P("tensor", "dp", None),
            P("tensor"),
            P("tensor"),
            P("tensor", None),
            P("tensor"),
            P(None, None, "tensor"),
            P(None, "tensor"),
            P("tensor"),
            P("tensor"),
            P("tensor", None),
            P("tensor"),
            P("tensor"),
            P("tensor"),
            P(None, "tensor", None),
            P(None, "tensor"),
            P(None, "tensor", None),
            P(None, "tensor"),
            P("tensor", None),
            P("tensor"),
        ),
        check_vma=False,
    )
```

profile of v0, /device:TPU:0, one launch (start us, length us, event | category | flops | bytes accessed | tf_op | source)
XLA Modules:
  0.0 2261.5 jit_solution(17377600485982242379)
XLA Ops:
  27.8 53.2 %all-gather.6.cloned.1.call-done = bf16[512,1,4096]{0,2,1:T(8,128)(2,1)} async-done(((bf16[256,1,4096]{0,2,1:T(8,128)(2,1)}), bf16[512,1,4096]{0,2,1:T(8,128)(2,1)}) %all-gather.6.cloned.1.call-update) | async-done | bytes 4194320 | tf_op jit(solution)/shard_map/all_gather | solution.py:203
  147.0 47.4 %all-gather.12.cloned.1.call-done = bf16[512,4096]{0,1:T(8,128)(2,1)} async-done(((bf16[256,4096]{0,1:T(8,128)(2,1)}), bf16[512,4096]{0,1:T(8,128)(2,1)}) %all-gather.12.cloned.1.call-update) | async-done | bytes 4194320 | tf_op jit(solution)/shard_map/all_gather | solution.py:211
  257.5 51.8 %all-gather.8.cloned.1.call-done = bf16[512,1,4096]{0,2,1:T(8,128)(2,1)} async-done(((bf16[256,1,4096]{0,2,1:T(8,128)(2,1)}), bf16[512,1,4096]{0,2,1:T(8,128)(2,1)}) %all-gather.8.cloned.1.call-update) | async-done | bytes 4194320 | tf_op jit(solution)/shard_map/all_gather | solution.py:214
  322.8 393.9 %while.30 = (s32[]{:T(128)}, bf16[8,4,64,512]{3,2,1,0:T(8,128)(2,1)}, f32[8,4,512,1]{2,1,3,0:T(4,128)S(1)}, f32[8,4,512,1]{2,1,3,0:T(4,128)S(1)}, bf16[8,4,64,51...) while((s32[]{:T(128)}, ...), condition=%wide.region_15.16_spmd.clone, body=%wide.region_12.15_spmd.clone.sunk | while | flops 2390978560 | bytes 121079936 | solution.py:120
  716.7 922.0 %while.31 = (s32[]{:T(128)}, f32[4,64,4356]{2,1,0:T(8,128)}, f32[4,64,4356]{2,1,0:T(8,128)}, bf16[8,4,64,512]{3,2,1,0:T(8,128)(2,1)}, bf16[8,4,64,512]{3,2,1,0:T...) while((s32[]{:T(128)}, f32[4,64,4356]{2,1,0:T(8,128)}, ...), condition=%wide.region_19.20_spmd.clone, body=%wide.region_17.19_spmd.clone.sunk | while | flops 5804411904 | bytes 302971552 | solution.py:159
  735.2 30.3 %multiply_reduce_fusion.7 = (f32[4,512]{1,0:T(4,128)S(1)}, f32[4,512,4356]{1,2,0:T(8,128)}) fusion(f32[4,512,4356]{1,2,0:T(8,128)} %fusion.456, f32[4,512]{1,0:T(4,128)S(1)} %get-tuple-element.508, f32[4,512]{1,0:T(4,128)S(1)} %get-tuple-element.509, bf16[4,64,4356]{2,1,0:T(8,128)(2,1)} %get-tuple-element.570, ...), kind=kOutput, calls=%fused_computation.20.clone.1 | convolution fusion | flops 1195423744 | bytes 73890816 | tf_op jit(solution)/shard_map/while/body/eval_jaxpr/gdi,gdj->gij/dot_general | solution.py:98
  765.5 29.7 %multiply_convert_fusion.4 = bf16[4,512,4356]{1,2,0:T(8,128)(2,1)} fusion(f32[4,512,4356]{1,2,0:T(8,128)} %get-tuple-element.510, f32[4,512,4356]{1,2,0:T(8,128)} %fusion.456, f32[4,512]{1,0:T(4,128)S(1)} %get-tuple-element.511), kind=kLoop, calls=%fused_computation.19.clone.1 | loop fusion | flops 26763264 | bytes 89219072 | tf_op jit(solution)/shard_map/while/body/eval_jaxpr/convert_element_type | solution.py:146
  847.9 30.3 %multiply_reduce_fusion.7 = (f32[4,512]{1,0:T(4,128)S(1)}, f32[4,512,4356]{1,2,0:T(8,128)}) fusion(f32[4,512,4356]{1,2,0:T(8,128)} %fusion.456, f32[4,512]{1,0:T(4,128)S(1)} %get-tuple-element.508, f32[4,512]{1,0:T(4,128)S(1)} %get-tuple-element.509, bf16[4,64,4356]{2,1,0:T(8,128)(2,1)} %get-tuple-element.570, ...), kind=kOutput, calls=%fused_computation.20.clone.1 | convolution fusion | flops 1195423744 | bytes 73890816 | tf_op jit(solution)/shard_map/while/body/eval_jaxpr/gdi,gdj->gij/dot_general | solution.py:98
  878.1 29.7 %multiply_convert_fusion.4 = bf16[4,512,4356]{1,2,0:T(8,128)(2,1)} fusion(f32[4,512,4356]{1,2,0:T(8,128)} %get-tuple-element.510, f32[4,512,4356]{1,2,0:T(8,128)} %fusion.456, f32[4,512]{1,0:T(4,128)S(1)} %get-tuple-element.511), kind=kLoop, calls=%fused_computation.19.clone.1 | loop fusion | flops 26763264 | bytes 89219072 | tf_op jit(solution)/shard_map/while/body/eval_jaxpr/convert_element_type | solution.py:146
  963.4 30.3 %multiply_reduce_fusion.7 = (f32[4,512]{1,0:T(4,128)S(1)}, f32[4,512,4356]{1,2,0:T(8,128)}) fusion(f32[4,512,4356]{1,2,0:T(8,128)} %fusion.456, f32[4,512]{1,0:T(4,128)S(1)} %get-tuple-element.508, f32[4,512]{1,0:T(4,128)S(1)} %get-tuple-element.509, bf16[4,64,4356]{2,1,0:T(8,128)(2,1)} %get-tuple-element.570, ...), kind=kOutput, calls=%fused_computation.20.clone.1 | convolution fusion | flops 1195423744 | bytes 73890816 | tf_op jit(solution)/shard_map/while/body/eval_jaxpr/gdi,gdj->gij/dot_general | solution.py:98
  993.7 29.7 %multiply_convert_fusion.4 = bf16[4,512,4356]{1,2,0:T(8,128)(2,1)} fusion(f32[4,512,4356]{1,2,0:T(8,128)} %get-tuple-element.510, f32[4,512,4356]{1,2,0:T(8,128)} %fusion.456, f32[4,512]{1,0:T(4,128)S(1)} %get-tuple-element.511), kind=kLoop, calls=%fused_computation.19.clone.1 | loop fusion | flops 26763264 | bytes 89219072 | tf_op jit(solution)/shard_map/while/body/eval_jaxpr/convert_element_type | solution.py:146
  1079.0 30.3 %multiply_reduce_fusion.7 = (f32[4,512]{1,0:T(4,128)S(1)}, f32[4,512,4356]{1,2,0:T(8,128)}) fusion(f32[4,512,4356]{1,2,0:T(8,128)} %fusion.456, f32[4,512]{1,0:T(4,128)S(1)} %get-tuple-element.508, f32[4,512]{1,0:T(4,128)S(1)} %get-tuple-element.509, bf16[4,64,4356]{2,1,0:T(8,128)(2,1)} %get-tuple-element.570, ...), kind=kOutput, calls=%fused_computation.20.clone.1 | convolution fusion | flops 1195423744 | bytes 73890816 | tf_op jit(solution)/shard_map/while/body/eval_jaxpr/gdi,gdj->gij/dot_general | solution.py:98
  1109.2 29.7 %multiply_convert_fusion.4 = bf16[4,512,4356]{1,2,0:T(8,128)(2,1)} fusion(f32[4,512,4356]{1,2,0:T(8,128)} %get-tuple-element.510, f32[4,512,4356]{1,2,0:T(8,128)} %fusion.456, f32[4,512]{1,0:T(4,128)S(1)} %get-tuple-element.511), kind=kLoop, calls=%fused_computation.19.clone.1 | loop fusion | flops 26763264 | bytes 89219072 | tf_op jit(solution)/shard_map/while/body/eval_jaxpr/convert_element_type | solution.py:146
  1194.5 30.3 %multiply_reduce_fusion.7 = (f32[4,512]{1,0:T(4,128)S(1)}, f32[4,512,4356]{1,2,0:T(8,128)}) fusion(f32[4,512,4356]{1,2,0:T(8,128)} %fusion.456, f32[4,512]{1,0:T(4,128)S(1)} %get-tuple-element.508, f32[4,512]{1,0:T(4,128)S(1)} %get-tuple-element.509, bf16[4,64,4356]{2,1,0:T(8,128)(2,1)} %get-tuple-element.570, ...), kind=kOutput, calls=%fused_computation.20.clone.1 | convolution fusion | flops 1195423744 | bytes 73890816 | tf_op jit(solution)/shard_map/while/body/eval_jaxpr/gdi,gdj->gij/dot_general | solution.py:98
  1224.8 29.7 %multiply_convert_fusion.4 = bf16[4,512,4356]{1,2,0:T(8,128)(2,1)} fusion(f32[4,512,4356]{1,2,0:T(8,128)} %get-tuple-element.510, f32[4,512,4356]{1,2,0:T(8,128)} %fusion.456, f32[4,512]{1,0:T(4,128)S(1)} %get-tuple-element.511), kind=kLoop, calls=%fused_computation.19.clone.1 | loop fusion | flops 26763264 | bytes 89219072 | tf_op jit(solution)/shard_map/while/body/eval_jaxpr/convert_element_type | solution.py:146
  1310.1 30.3 %multiply_reduce_fusion.7 = (f32[4,512]{1,0:T(4,128)S(1)}, f32[4,512,4356]{1,2,0:T(8,128)}) fusion(f32[4,512,4356]{1,2,0:T(8,128)} %fusion.456, f32[4,512]{1,0:T(4,128)S(1)} %get-tuple-element.508, f32[4,512]{1,0:T(4,128)S(1)} %get-tuple-element.509, bf16[4,64,4356]{2,1,0:T(8,128)(2,1)} %get-tuple-element.570, ...), kind=kOutput, calls=%fused_computation.20.clone.1 | convolution fusion | flops 1195423744 | bytes 73890816 | tf_op jit(solution)/shard_map/while/body/eval_jaxpr/gdi,gdj->gij/dot_general | solution.py:98
  1340.3 29.7 %multiply_convert_fusion.4 = bf16[4,512,4356]{1,2,0:T(8,128)(2,1)} fusion(f32[4,512,4356]{1,2,0:T(8,128)} %get-tuple-element.510, f32[4,512,4356]{1,2,0:T(8,128)} %fusion.456, f32[4,512]{1,0:T(4,128)S(1)} %get-tuple-element.511), kind=kLoop, calls=%fused_computation.19.clone.1 | loop fusion | flops 26763264 | bytes 89219072 | tf_op jit(solution)/shard_map/while/body/eval_jaxpr/convert_element_type | solution.py:146
  1425.6 30.3 %multiply_reduce_fusion.7 = (f32[4,512]{1,0:T(4,128)S(1)}, f32[4,512,4356]{1,2,0:T(8,128)}) fusion(f32[4,512,4356]{1,2,0:T(8,128)} %fusion.456, f32[4,512]{1,0:T(4,128)S(1)} %get-tuple-element.508, f32[4,512]{1,0:T(4,128)S(1)} %get-tuple-element.509, bf16[4,64,4356]{2,1,0:T(8,128)(2,1)} %get-tuple-element.570, ...), kind=kOutput, calls=%fused_computation.20.clone.1 | convolution fusion | flops 1195423744 | bytes 73890816 | tf_op jit(solution)/shard_map/while/body/eval_jaxpr/gdi,gdj->gij/dot_general | solution.py:98
  1455.9 29.7 %multiply_convert_fusion.4 = bf16[4,512,4356]{1,2,0:T(8,128)(2,1)} fusion(f32[4,512,4356]{1,2,0:T(8,128)} %get-tuple-element.510, f32[4,512,4356]{1,2,0:T(8,128)} %fusion.456, f32[4,512]{1,0:T(4,128)S(1)} %get-tuple-element.511), kind=kLoop, calls=%fused_computation.19.clone.1 | loop fusion | flops 26763264 | bytes 89219072 | tf_op jit(solution)/shard_map/while/body/eval_jaxpr/convert_element_type | solution.py:146
  1541.1 30.3 %multiply_reduce_fusion.7 = (f32[4,512]{1,0:T(4,128)S(1)}, f32[4,512,4356]{1,2,0:T(8,128)}) fusion(f32[4,512,4356]{1,2,0:T(8,128)} %fusion.456, f32[4,512]{1,0:T(4,128)S(1)} %get-tuple-element.508, f32[4,512]{1,0:T(4,128)S(1)} %get-tuple-element.509, bf16[4,64,4356]{2,1,0:T(8,128)(2,1)} %get-tuple-element.570, ...), kind=kOutput, calls=%fused_computation.20.clone.1 | convolution fusion | flops 1195423744 | bytes 73890816 | tf_op jit(solution)/shard_map/while/body/eval_jaxpr/gdi,gdj->gij/dot_general | solution.py:98
  1683.3 45.2 %reduce-scatter.7.cloned.1.call-done = bf16[256,1,4096]{0,2,1:T(8,128)(2,1)} async-done(((bf16[512,1,4096]{0,2,1:T(8,128)(2,1)}), bf16[256,1,4096]{0,2,1:T(8,128)(2,1)}) %reduce-scatter.7.cloned.1.call-update) | async-done | bytes 2097168 | tf_op jit(solution)/shard_map/reduce_scatter | solution.py:276
  2012.0 119.1 %all-reduce.10.cloned.1.call-done = (bf16[256,4608]{0,1:T(8,128)(2,1)}, bf16[256,4608]{0,1:T(8,128)(2,1)}, bf16[256,512]{0,1:T(8,128)(2,1)}, bf16[2,2048,256]{2,...) async-done(((bf16[256,4608]{0,1:T(8,128)(2,1)}, bf16[256,4608]{0,1:T(8,128)(2,1)}, bf16[256,512]{0,1:T(8,128)(2,1)}, ...) | async-done | bytes 9961488 | tf_op jit(solution)/shard_map/psum | solution.py:318
  2147.7 40.5 %reduce-scatter.11.cloned.1.call-done = bf16[256,1,4096]{0,2,1:T(8,128)(2,1)} async-done(((bf16[512,1,4096]{0,2,1:T(8,128)(2,1)}), bf16[256,1,4096]{0,2,1:T(8,128)(2,1)}) %reduce-scatter.11.cloned.1.call-update) | async-done | bytes 2097168 | tf_op jit(solution)/shard_map/reduce_scatter | solution.py:73
  2194.1 34.2 %all-reduce.6 = (bf16[256]{0:T(256)(128)(2,1)S(1)}, bf16[256]{0:T(256)(128)(2,1)S(1)}, bf16[256]{0:T(256)(128)(2,1)S(1)}, bf16[2,256]{1,0:T(2,128)(2,1)S(1)}, bf...) all-reduce(bf16[256]{0:T(256)(128)(2,1)S(1)} %get-tuple-element.252, ...), channel_id=1, replica_groups=mesh['dp'=16,'tensor'=2] {'dp'}, use_global_device_ids=true, to_apply=%region_42.43 | all-reduce | flops 4096 | bytes 16384 | tf_op jit(solution)/shard_map/psum | solution.py:316
  (563 shorter events, 1402.8 us)
Async XLA Ops:
  7.2 243.3 %copy-start = (bf16[2,256,2048]{2,1,0:T(8,128)(2,1)S(1)}, bf16[2,256,2048]{2,1,0:T(8,128)(2,1)}, u32[]{:S(2)}) copy-start(bf16[2,256,2048]{2,1,0:T(8,128)(2,1)} %param.46) | copy-start | bytes 6291460
  7.2 73.8 %all-gather.6.cloned.1.call-start = ((), (), s32[]{:S(2)}) async-start(), calls=%async_computation.4 | async-start | bytes 6291456 | tf_op jit(solution)/shard_map/all_gather | solution.py:203
  21.5 173.0 %all-gather.12.cloned.1.call-start = ((), (), s32[]{:S(2)}) async-start(), calls=%async_computation.11 | async-start | bytes 6291456 | tf_op jit(solution)/shard_map/all_gather | solution.py:211
  27.8 104.4 %copy-start.72 = (f32[1,256]{1,0:T(1,128)}, f32[1,256]{1,0:T(1,128)S(1)}, u32[]{:S(2)}) copy-start(f32[1,256]{1,0:T(1,128)S(1)} %get-tuple-element.370) | copy-start | bytes 3076
  27.8 104.4 %copy-start.88 = (f32[1,256]{1,0:T(1,128)}, f32[1,256]{1,0:T(1,128)S(1)}, u32[]{:S(2)}) copy-start(f32[1,256]{1,0:T(1,128)S(1)} %get-tuple-element.371) | copy-start | bytes 3076
  137.6 116.1 %reduce-scatter.5.cloned.1.call-start = ((), (), s32[]{:S(2)}) async-start(), calls=%async_computation.7 | async-start | bytes 6291456 | tf_op jit(solution)/shard_map/reduce_scatter | solution.py:246
  142.5 166.8 %all-gather.8.cloned.1.call-start = ((), (), s32[]{:S(2)}) async-start(), calls=%async_computation.5 | async-start | bytes 6291456 | tf_op jit(solution)/shard_map/all_gather | solution.py:214
  250.3 1478.1 %reduce-scatter.7.cloned.1.call-start = ((), (), s32[]{:S(2)}) async-start(), calls=%async_computation.8 | async-start | bytes 6291456 | tf_op jit(solution)/shard_map/reduce_scatter | solution.py:276
  250.5 58.8 %copy-start.110 = (bf16[3,256,512]{2,1,0:T(8,128)(2,1)S(1)}, bf16[3,256,512]{2,1,0:T(8,128)(2,1)}, u32[]{:S(2)}) copy-start(bf16[3,256,512]{2,1,0:T(8,128)(2,1)} %param.44) | copy-start | bytes 2359300
  250.5 58.8 %copy-start.112 = (f32[3,256]{1,0:T(4,128)S(1)}, f32[3,256]{1,0:T(4,128)}, u32[]{:S(2)}) copy-start(f32[3,256]{1,0:T(4,128)} %param.45) | copy-start | bytes 9220
  1674.0 154.9 %all-gather.10.cloned.1.call-start = ((), (), s32[]{:S(2)}) async-start(), calls=%async_computation.6 | async-start | bytes 6291456 | tf_op jit(solution)/shard_map/all_gather | solution.py:234
  1680.8 47.7 %copy-start.62 = (f32[256]{0:T(256)S(1)}, f32[256]{0:T(256)}, u32[]{:S(2)}) copy-start(f32[256]{0:T(256)} %copy-done.61) | copy-start | bytes 3076
  1680.8 47.7 %copy-start.75 = (f32[256]{0:T(256)S(1)}, f32[256]{0:T(256)}, u32[]{:S(2)}) copy-start(f32[256]{0:T(256)} %copy-done.74) | copy-start | bytes 3076
  1680.8 47.7 %copy-start.84 = (f32[256]{0:T(256)S(1)}, f32[256]{0:T(256)}, u32[]{:S(2)}) copy-start(f32[256]{0:T(256)} %param.42) | copy-start | bytes 3076
  1683.2 50.2 %copy-start.109 = (f32[16]{0:T(128)S(1)}, f32[16]{0:T(128)}, u32[]{:S(2)}) copy-start(f32[16]{0:T(128)} %copy-done.108) | copy-start | bytes 196
  1683.2 185.0 %reduce-scatter.9.cloned.1.call-start = ((), (), s32[]{:S(2)}) async-start(), calls=%async_computation.9 | async-start | bytes 6291456 | tf_op jit(solution)/shard_map/reduce_scatter | solution.py:73
  1813.6 317.5 %all-reduce.10.cloned.1.call-start = ((), (), s32[]{:S(2)}) async-start(), calls=%async_computation.12 | async-start | bytes 19922944 | tf_op jit(solution)/shard_map/psum | solution.py:318
  1935.5 252.7 %reduce-scatter.11.cloned.1.call-start = ((), (), s32[]{:S(2)}) async-start(), calls=%async_computation.10 | async-start | bytes 6291456 | tf_op jit(solution)/shard_map/reduce_scatter | solution.py:73
  2147.6 87.7 %copy-start.105 = (f32[16]{0:T(128)S(1)}, f32[16]{0:T(128)}, u32[]{:S(2)}) copy-start(f32[16]{0:T(128)} %copy-done.104) | copy-start | bytes 196
  2147.6 89.0 %copy-start.63 = (f32[256]{0:T(256)S(1)}, f32[256]{0:T(256)}, u32[]{:S(2)}) copy-start(f32[256]{0:T(256)} %copy-done.61) | copy-start | bytes 3076
  2147.6 89.0 %copy-start.76 = (f32[256]{0:T(256)S(1)}, f32[256]{0:T(256)}, u32[]{:S(2)}) copy-start(f32[256]{0:T(256)} %copy-done.74) | copy-start | bytes 3076
  2147.7 89.0 %copy-start.82 = (f32[256]{0:T(256)S(1)}, f32[256]{0:T(256)}, u32[]{:S(2)}) copy-start(f32[256]{0:T(256)} %copy-done.81) | copy-start | bytes 3076
  2147.7 89.0 %copy-start.85 = (f32[256]{0:T(256)S(1)}, f32[256]{0:T(256)}, u32[]{:S(2)}) copy-start(f32[256]{0:T(256)} %param.42) | copy-start | bytes 3076
  2147.7 89.0 %copy-start.91 = (f32[256]{0:T(256)S(1)}, f32[256]{0:T(256)}, u32[]{:S(2)}) copy-start(f32[256]{0:T(256)} %copy-done.90) | copy-start | bytes 3076
  (113 other events, 1221.3 us)
Sparse Core Ops, SparseCore 0:
  21.6 59.4 all-gather.5
  137.7 56.7 all-gather.11
  196.8 54.2 reduce-scatter.4
  252.5 56.7 all-gather.7
  1674.1 54.3 reduce-scatter.6
  1730.5 56.7 all-gather.9
  1813.7 54.4 reduce-scatter.8
  1935.6 195.4 all-reduce.9
  2134.0 54.1 reduce-scatter.10
where the time goes:
time: 2270 us; the launch traced here: 2260 us
  matrix products  1190 us (52%)
  other arithmetic  460 us (20%)
  waiting for transfers between devices  367 us (16%)
  local copies, waits for them, and re-layouts  189 us (8%)
  blocking collectives  34.2 us (2%)
    dot_general x16, matrix products, masked_scores(): jnp.einsum('gdi,gdj->gij', q_block, key_rows, preferred_element_type=jnp....  378 us
    convert_element_type x8, other arithmetic, one_block(): grad_scores = (prob_f32 * (grad_probs - delta_row)).astype(jnp.bfloat16)  238 us
    dot_general x8, matrix products, one_block(): jnp.einsum('gdi,gdj->gij', g_block, value_rows, preferred_element_type=jn...  147 us
    dot_general x8, matrix products, one_block(): jnp.einsum('gdi,gij->gdj', g_block, probs_low, preferred_element_type=jnp...  134 us
    dot_general x18, matrix products, conv_input_grad(): jnp.einsum('oc,oip->cip', cols_part, moved_grads[kernel_tap], preferred_e...  131 us
    reduce_sum x8, other arithmetic, one_block(): row_total = jnp.sum(raised, axis=-1, keepdims=True)  130 us
    dot_general x8, matrix products, one_block(): jnp.einsum('gdj,gij->gdi', value_rows, probs_low, preferred_element_type=...  128 us
    psum x1, waiting for transfers between devices, local(): lax.psum(conv1_weight_grad.astype(jnp.bfloat16), 'dp').astype(jnp.float32)  119 us
  transfers between devices with their start and end apart: 9, of which 7 were waited for; matrix products, arithmetic and copies ran while one was open for 13% of the time, Pallas kernels for 0%

commit v1 on v0

--- a/solution.py
+++ b/solution.py
@@ -11,6 +11,11 @@
 CTX = 260
 EPSILON = 1e-05
 NEG_FILL = -1e30
+
+
+def add_all(x, name):
+    blocks = lax.all_gather(x, name)
+    return jnp.sum(blocks, axis=0)
 
 
 def group_norm(values, gain_vec, bias_vec):
@@ -315,7 +320,7 @@
     residual_grads = (
         lax.psum(norm1_gain_grad.astype(jnp.bfloat16), "dp").astype(jnp.float32),
         lax.psum(norm1_bias_grad.astype(jnp.bfloat16), "dp").astype(jnp.float32),
-        lax.psum(conv1_weight_grad.astype(jnp.bfloat16), "dp").astype(jnp.float32),
+        add_all(conv1_weight_grad.astype(jnp.bfloat16), "dp").astype(jnp.float32),
         lax.psum(conv1_bias_grad.astype(jnp.bfloat16), "dp").astype(jnp.float32),
         lax.psum(emb_weight_grad.astype(jnp.bfloat16), "dp").astype(jnp.float32),
         lax.psum(emb_bias_grad.astype(jnp.bfloat16), "dp").astype(jnp.float32),

time: 2270 us -> 2380 us (1.048)
  waiting for transfers between devices: 367 us -> 441 us
  other arithmetic: 460 us -> 487 us
    all_gather x0 -> x1, waiting for transfers between devices: none -> 123 us  [add_all(): blocks = lax.all_gather(x, name)]
    psum x1, waiting for transfers between devices: 119 us -> 66 us  [local(): lax.psum(conv2_weight_grad.astype(jnp.bfloat16), 'dp').astype(jnp.float32)]
    unnamed x235 -> x230, local copies, waits for them, and re-layouts: 68.7 us -> 71.1 us
  transfers between devices with their start and end apart: 9 -> 10, of which waited for: 7 -> 8; matrix products, arithmetic and copies ran while one was open for 13% -> 14% of each run, Pallas kernels for 0% -> 0%
where the time goes in v1:
time: 2380 us; the launch traced here: 2370 us
  matrix products  1190 us (50%)
  other arithmetic  487 us (20%)
  waiting for transfers between devices  441 us (19%)
  local copies, waits for them, and re-layouts  196 us (8%)
  blocking collectives  36.1 us (2%)
    dot_general x16, matrix products, masked_scores(): jnp.einsum('gdi,gdj->gij', q_block, key_rows, preferred_element_type=jnp....  378 us
    convert_element_type x8, other arithmetic, one_block(): grad_scores = (prob_f32 * (grad_probs - delta_row)).astype(jnp.bfloat16)  238 us
    dot_general x8, matrix products, one_block(): jnp.einsum('gdi,gdj->gij', g_block, value_rows, preferred_element_type=jn...  147 us
    dot_general x8, matrix products, one_block(): jnp.einsum('gdi,gij->gdj', g_block, probs_low, preferred_element_type=jnp...  134 us
    reduce_sum x8, other arithmetic, one_block(): row_total = jnp.sum(raised, axis=-1, keepdims=True)  130 us
    dot_general x8, matrix products, one_block(): jnp.einsum('gdj,gij->gdi', value_rows, probs_low, preferred_element_type=...  128 us
    dot_general x18, matrix products, conv_input_grad(): jnp.einsum('oc,oip->cip', cols_part, moved_grads[kernel_tap], preferred_e...  126 us
    all_gather x1, waiting for transfers between devices, add_all(): blocks = lax.all_gather(x, name)  123 us
  transfers between devices with their start and end apart: 10, of which 8 were waited for; matrix products, arithmetic and copies ran while one was open for 14% of the time, Pallas kernels for 0%

profile of v1, /device:TPU:0, one launch (start us, length us, event | category | flops | bytes accessed | tf_op | source)
XLA Modules:
  0.0 2369.9 jit_solution(2276478470253049825)
XLA Ops:
  27.9 53.2 %all-gather.7.cloned.1.call-done = bf16[512,1,4096]{0,2,1:T(8,128)(2,1)} async-done(((bf16[256,1,4096]{0,2,1:T(8,128)(2,1)}), bf16[512,1,4096]{0,2,1:T(8,128)(2,1)}) %all-gather.7.cloned.1.call-update) | async-done | bytes 4194320 | tf_op jit(solution)/shard_map/all_gather | solution.py:208
  159.5 47.5 %all-gather.15.cloned.1.call-done = bf16[512,4096]{0,1:T(8,128)(2,1)} async-done(((bf16[256,4096]{0,1:T(8,128)(2,1)}), bf16[512,4096]{0,1:T(8,128)(2,1)}) %all-gather.15.cloned.1.call-update) | async-done | bytes 4194320 | tf_op jit(solution)/shard_map/all_gather | solution.py:216
  269.9 51.9 %all-gather.9.cloned.1.call-done = bf16[512,1,4096]{0,2,1:T(8,128)(2,1)} async-done(((bf16[256,1,4096]{0,2,1:T(8,128)(2,1)}), bf16[512,1,4096]{0,2,1:T(8,128)(2,1)}) %all-gather.9.cloned.1.call-update) | async-done | bytes 4194320 | tf_op jit(solution)/shard_map/all_gather | solution.py:219
  335.3 394.0 %while.30 = (s32[]{:T(128)}, bf16[8,4,64,512]{3,2,1,0:T(8,128)(2,1)}, f32[8,4,512,1]{2,1,3,0:T(4,128)S(1)}, f32[8,4,512,1]{2,1,3,0:T(4,128)S(1)}, bf16[8,4,64,51...) while((s32[]{:T(128)}, ...), condition=%wide.region_15.16_spmd.clone, body=%wide.region_12.15_spmd.clone.sunk | while | flops 2390978560 | bytes 121079936 | solution.py:125
  729.3 921.8 %while.31 = (s32[]{:T(128)}, f32[4,64,4356]{2,1,0:T(8,128)}, f32[4,64,4356]{2,1,0:T(8,128)}, bf16[8,4,64,512]{3,2,1,0:T(8,128)(2,1)}, bf16[8,4,64,512]{3,2,1,0:T...) while((s32[]{:T(128)}, f32[4,64,4356]{2,1,0:T(8,128)}, ...), condition=%wide.region_19.20_spmd.clone, body=%wide.region_17.19_spmd.clone.sunk | while | flops 5804411904 | bytes 302971552 | solution.py:164
  747.8 30.3 %multiply_reduce_fusion.7 = (f32[4,512]{1,0:T(4,128)S(1)}, f32[4,512,4356]{1,2,0:T(8,128)}) fusion(f32[4,512,4356]{1,2,0:T(8,128)} %fusion.456, f32[4,512]{1,0:T(4,128)S(1)} %get-tuple-element.527, f32[4,512]{1,0:T(4,128)S(1)} %get-tuple-element.528, bf16[4,64,4356]{2,1,0:T(8,128)(2,1)} %get-tuple-element.589, ...), kind=kOutput, calls=%fused_computation.20.clone.1 | convolution fusion | flops 1195423744 | bytes 73890816 | tf_op jit(solution)/shard_map/while/body/eval_jaxpr/gdi,gdj->gij/dot_general | solution.py:103
  778.1 29.7 %multiply_convert_fusion.4 = bf16[4,512,4356]{1,2,0:T(8,128)(2,1)} fusion(f32[4,512,4356]{1,2,0:T(8,128)} %get-tuple-element.529, f32[4,512,4356]{1,2,0:T(8,128)} %fusion.456, f32[4,512]{1,0:T(4,128)S(1)} %get-tuple-element.530), kind=kLoop, calls=%fused_computation.19.clone.1 | loop fusion | flops 26763264 | bytes 89219072 | tf_op jit(solution)/shard_map/while/body/eval_jaxpr/convert_element_type | solution.py:151
  860.4 30.3 %multiply_reduce_fusion.7 = (f32[4,512]{1,0:T(4,128)S(1)}, f32[4,512,4356]{1,2,0:T(8,128)}) fusion(f32[4,512,4356]{1,2,0:T(8,128)} %fusion.456, f32[4,512]{1,0:T(4,128)S(1)} %get-tuple-element.527, f32[4,512]{1,0:T(4,128)S(1)} %get-tuple-element.528, bf16[4,64,4356]{2,1,0:T(8,128)(2,1)} %get-tuple-element.589, ...), kind=kOutput, calls=%fused_computation.20.clone.1 | convolution fusion | flops 1195423744 | bytes 73890816 | tf_op jit(solution)/shard_map/while/body/eval_jaxpr/gdi,gdj->gij/dot_general | solution.py:103
  890.7 29.7 %multiply_convert_fusion.4 = bf16[4,512,4356]{1,2,0:T(8,128)(2,1)} fusion(f32[4,512,4356]{1,2,0:T(8,128)} %get-tuple-element.529, f32[4,512,4356]{1,2,0:T(8,128)} %fusion.456, f32[4,512]{1,0:T(4,128)S(1)} %get-tuple-element.530), kind=kLoop, calls=%fused_computation.19.clone.1 | loop fusion | flops 26763264 | bytes 89219072 | tf_op jit(solution)/shard_map/while/body/eval_jaxpr/convert_element_type | solution.py:151
  976.0 30.3 %multiply_reduce_fusion.7 = (f32[4,512]{1,0:T(4,128)S(1)}, f32[4,512,4356]{1,2,0:T(8,128)}) fusion(f32[4,512,4356]{1,2,0:T(8,128)} %fusion.456, f32[4,512]{1,0:T(4,128)S(1)} %get-tuple-element.527, f32[4,512]{1,0:T(4,128)S(1)} %get-tuple-element.528, bf16[4,64,4356]{2,1,0:T(8,128)(2,1)} %get-tuple-element.589, ...), kind=kOutput, calls=%fused_computation.20.clone.1 | convolution fusion | flops 1195423744 | bytes 73890816 | tf_op jit(solution)/shard_map/while/body/eval_jaxpr/gdi,gdj->gij/dot_general | solution.py:103
  1006.2 29.7 %multiply_convert_fusion.4 = bf16[4,512,4356]{1,2,0:T(8,128)(2,1)} fusion(f32[4,512,4356]{1,2,0:T(8,128)} %get-tuple-element.529, f32[4,512,4356]{1,2,0:T(8,128)} %fusion.456, f32[4,512]{1,0:T(4,128)S(1)} %get-tuple-element.530), kind=kLoop, calls=%fused_computation.19.clone.1 | loop fusion | flops 26763264 | bytes 89219072 | tf_op jit(solution)/shard_map/while/body/eval_jaxpr/convert_element_type | solution.py:151
  1091.5 30.3 %multiply_reduce_fusion.7 = (f32[4,512]{1,0:T(4,128)S(1)}, f32[4,512,4356]{1,2,0:T(8,128)}) fusion(f32[4,512,4356]{1,2,0:T(8,128)} %fusion.456, f32[4,512]{1,0:T(4,128)S(1)} %get-tuple-element.527, f32[4,512]{1,0:T(4,128)S(1)} %get-tuple-element.528, bf16[4,64,4356]{2,1,0:T(8,128)(2,1)} %get-tuple-element.589, ...), kind=kOutput, calls=%fused_computation.20.clone.1 | convolution fusion | flops 1195423744 | bytes 73890816 | tf_op jit(solution)/shard_map/while/body/eval_jaxpr/gdi,gdj->gij/dot_general | solution.py:103
  1121.8 29.7 %multiply_convert_fusion.4 = bf16[4,512,4356]{1,2,0:T(8,128)(2,1)} fusion(f32[4,512,4356]{1,2,0:T(8,128)} %get-tuple-element.529, f32[4,512,4356]{1,2,0:T(8,128)} %fusion.456, f32[4,512]{1,0:T(4,128)S(1)} %get-tuple-element.530), kind=kLoop, calls=%fused_computation.19.clone.1 | loop fusion | flops 26763264 | bytes 89219072 | tf_op jit(solution)/shard_map/while/body/eval_jaxpr/convert_element_type | solution.py:151
  1207.0 30.3 %multiply_reduce_fusion.7 = (f32[4,512]{1,0:T(4,128)S(1)}, f32[4,512,4356]{1,2,0:T(8,128)}) fusion(f32[4,512,4356]{1,2,0:T(8,128)} %fusion.456, f32[4,512]{1,0:T(4,128)S(1)} %get-tuple-element.527, f32[4,512]{1,0:T(4,128)S(1)} %get-tuple-element.528, bf16[4,64,4356]{2,1,0:T(8,128)(2,1)} %get-tuple-element.589, ...), kind=kOutput, calls=%fused_computation.20.clone.1 | convolution fusion | flops 1195423744 | bytes 73890816 | tf_op jit(solution)/shard_map/while/body/eval_jaxpr/gdi,gdj->gij/dot_general | solution.py:103
  1237.3 29.7 %multiply_convert_fusion.4 = bf16[4,512,4356]{1,2,0:T(8,128)(2,1)} fusion(f32[4,512,4356]{1,2,0:T(8,128)} %get-tuple-element.529, f32[4,512,4356]{1,2,0:T(8,128)} %fusion.456, f32[4,512]{1,0:T(4,128)S(1)} %get-tuple-element.530), kind=kLoop, calls=%fused_computation.19.clone.1 | loop fusion | flops 26763264 | bytes 89219072 | tf_op jit(solution)/shard_map/while/body/eval_jaxpr/convert_element_type | solution.py:151
  1322.5 30.3 %multiply_reduce_fusion.7 = (f32[4,512]{1,0:T(4,128)S(1)}, f32[4,512,4356]{1,2,0:T(8,128)}) fusion(f32[4,512,4356]{1,2,0:T(8,128)} %fusion.456, f32[4,512]{1,0:T(4,128)S(1)} %get-tuple-element.527, f32[4,512]{1,0:T(4,128)S(1)} %get-tuple-element.528, bf16[4,64,4356]{2,1,0:T(8,128)(2,1)} %get-tuple-element.589, ...), kind=kOutput, calls=%fused_computation.20.clone.1 | convolution fusion | flops 1195423744 | bytes 73890816 | tf_op jit(solution)/shard_map/while/body/eval_jaxpr/gdi,gdj->gij/dot_general | solution.py:103
  1438.1 30.3 %multiply_reduce_fusion.7 = (f32[4,512]{1,0:T(4,128)S(1)}, f32[4,512,4356]{1,2,0:T(8,128)}) fusion(f32[4,512,4356]{1,2,0:T(8,128)} %fusion.456, f32[4,512]{1,0:T(4,128)S(1)} %get-tuple-element.527, f32[4,512]{1,0:T(4,128)S(1)} %get-tuple-element.528, bf16[4,64,4356]{2,1,0:T(8,128)(2,1)} %get-tuple-element.589, ...), kind=kOutput, calls=%fused_computation.20.clone.1 | convolution fusion | flops 1195423744 | bytes 73890816 | tf_op jit(solution)/shard_map/while/body/eval_jaxpr/gdi,gdj->gij/dot_general | solution.py:103
  1468.4 29.7 %multiply_convert_fusion.4 = bf16[4,512,4356]{1,2,0:T(8,128)(2,1)} fusion(f32[4,512,4356]{1,2,0:T(8,128)} %get-tuple-element.529, f32[4,512,4356]{1,2,0:T(8,128)} %fusion.456, f32[4,512]{1,0:T(4,128)S(1)} %get-tuple-element.530), kind=kLoop, calls=%fused_computation.19.clone.1 | loop fusion | flops 26763264 | bytes 89219072 | tf_op jit(solution)/shard_map/while/body/eval_jaxpr/convert_element_type | solution.py:151
  1553.6 30.3 %multiply_reduce_fusion.7 = (f32[4,512]{1,0:T(4,128)S(1)}, f32[4,512,4356]{1,2,0:T(8,128)}) fusion(f32[4,512,4356]{1,2,0:T(8,128)} %fusion.456, f32[4,512]{1,0:T(4,128)S(1)} %get-tuple-element.527, f32[4,512]{1,0:T(4,128)S(1)} %get-tuple-element.528, bf16[4,64,4356]{2,1,0:T(8,128)(2,1)} %get-tuple-element.589, ...), kind=kOutput, calls=%fused_computation.20.clone.1 | convolution fusion | flops 1195423744 | bytes 73890816 | tf_op jit(solution)/shard_map/while/body/eval_jaxpr/gdi,gdj->gij/dot_general | solution.py:103
  1695.5 45.2 %reduce-scatter.7.cloned.1.call-done = bf16[256,1,4096]{0,2,1:T(8,128)(2,1)} async-done(((bf16[512,1,4096]{0,2,1:T(8,128)(2,1)}), bf16[256,1,4096]{0,2,1:T(8,128)(2,1)}) %reduce-scatter.7.cloned.1.call-update) | async-done | bytes 2097168 | tf_op jit(solution)/shard_map/reduce_scatter | solution.py:281
  2025.1 66.0 %all-reduce.10.cloned.1.call-done = (bf16[256,4608]{0,1:T(8,128)(2,1)}, bf16[256,512]{0,1:T(8,128)(2,1)}, bf16[2,2048,256]{2,1,0:T(8,128)(2,1)}, bf16[3,256,512]{2,1,0:T(8,128)(2,1)}, bf16[2,256,2048]{2,1,0:T(8,128)(2,1)}) async-done(((bf16[256,4608]{0,1:T(8,128)(2,1)}, bf16[256,512]{0,1:T(8,128)(2,1)}, bf16[2,2048,256]{2,1,0:T(8,128)(2,1)}, bf16[3,256,512]{2,1,0:T(8,128)(2,1)}, ...) | async-done | bytes 7602192 | tf_op jit(solution)/shard_map/psum | solution.py:329
  2103.0 45.0 %reduce-scatter.11.cloned.1.call-done = bf16[256,1,4096]{0,2,1:T(8,128)(2,1)} async-done(((bf16[512,1,4096]{0,2,1:T(8,128)(2,1)}), bf16[256,1,4096]{0,2,1:T(8,128)(2,1)}) %reduce-scatter.11.cloned.1.call-update) | async-done | bytes 2097168 | tf_op jit(solution)/shard_map/reduce_scatter | solution.py:78
  2154.0 36.1 %all-reduce.6 = (bf16[256]{0:T(256)(128)(2,1)S(1)}, bf16[256]{0:T(256)(128)(2,1)S(1)}, bf16[256]{0:T(256)(128)(2,1)S(1)}, bf16[2,256]{1,0:T(2,128)(2,1)S(1)}, bf...) all-reduce(bf16[256]{0:T(256)(128)(2,1)S(1)} %get-tuple-element.272, ...), channel_id=1, replica_groups=mesh['dp'=16,'tensor'=2] {'dp'}, use_global_device_ids=true, to_apply=%region_42.43 | all-reduce | flops 4096 | bytes 16384 | tf_op jit(solution)/shard_map/psum | solution.py:321
  2216.0 123.0 %all-gather.13.cloned.1.call-done = bf16[16,256,4608]{2,1,0:T(8,128)(2,1)} async-done(((bf16[1,256,4608]{2,1,0:T(8,128)(2,1)}), bf16[16,256,4608]{2,1,0:T(8,128)(2,1)}) %all-gather.13.cloned.1.call-update) | async-done | bytes 37748752 | tf_op jit(solution)/shard_map/all_gather | solution.py:17
  (563 shorter events, 1464.2 us)
Async XLA Ops:
  7.2 255.8 %copy-start = (bf16[2,256,2048]{2,1,0:T(8,128)(2,1)S(1)}, bf16[2,256,2048]{2,1,0:T(8,128)(2,1)}, u32[]{:S(2)}) copy-start(bf16[2,256,2048]{2,1,0:T(8,128)(2,1)} %param.46) | copy-start | bytes 6291460
  7.2 73.9 %all-gather.7.cloned.1.call-start = ((), (), s32[]{:S(2)}) async-start(), calls=%async_computation.4 | async-start | bytes 6291456 | tf_op jit(solution)/shard_map/all_gather | solution.py:208
  21.6 185.4 %all-gather.15.cloned.1.call-start = ((), (), s32[]{:S(2)}) async-start(), calls=%async_computation.12 | async-start | bytes 6291456 | tf_op jit(solution)/shard_map/all_gather | solution.py:216
  27.9 104.3 %copy-start.69 = (f32[1,256]{1,0:T(1,128)}, f32[1,256]{1,0:T(1,128)S(1)}, u32[]{:S(2)}) copy-start(f32[1,256]{1,0:T(1,128)S(1)} %get-tuple-element.389) | copy-start | bytes 3076
  27.9 104.3 %copy-start.85 = (f32[1,256]{1,0:T(1,128)}, f32[1,256]{1,0:T(1,128)S(1)}, u32[]{:S(2)}) copy-start(f32[1,256]{1,0:T(1,128)S(1)} %get-tuple-element.390) | copy-start | bytes 3076
  150.1 116.1 %reduce-scatter.5.cloned.1.call-start = ((), (), s32[]{:S(2)}) async-start(), calls=%async_computation.7 | async-start | bytes 6291456 | tf_op jit(solution)/shard_map/reduce_scatter | solution.py:251
  155.0 166.8 %all-gather.9.cloned.1.call-start = ((), (), s32[]{:S(2)}) async-start(), calls=%async_computation.5 | async-start | bytes 6291456 | tf_op jit(solution)/shard_map/all_gather | solution.py:219
  262.8 1477.9 %reduce-scatter.7.cloned.1.call-start = ((), (), s32[]{:S(2)}) async-start(), calls=%async_computation.8 | async-start | bytes 6291456 | tf_op jit(solution)/shard_map/reduce_scatter | solution.py:281
  263.0 58.8 %copy-start.107 = (bf16[3,256,512]{2,1,0:T(8,128)(2,1)S(1)}, bf16[3,256,512]{2,1,0:T(8,128)(2,1)}, u32[]{:S(2)}) copy-start(bf16[3,256,512]{2,1,0:T(8,128)(2,1)} %param.44) | copy-start | bytes 2359300
  263.0 58.8 %copy-start.109 = (f32[3,256]{1,0:T(4,128)S(1)}, f32[3,256]{1,0:T(4,128)}, u32[]{:S(2)}) copy-start(f32[3,256]{1,0:T(4,128)} %param.45) | copy-start | bytes 9220
  1686.3 154.7 %all-gather.11.cloned.1.call-start = ((), (), s32[]{:S(2)}) async-start(), calls=%async_computation.6 | async-start | bytes 6291456 | tf_op jit(solution)/shard_map/all_gather | solution.py:239
  1695.5 184.9 %reduce-scatter.9.cloned.1.call-start = ((), (), s32[]{:S(2)}) async-start(), calls=%async_computation.9 | async-start | bytes 6291456 | tf_op jit(solution)/shard_map/reduce_scatter | solution.py:78
  1825.8 265.2 %all-reduce.10.cloned.1.call-start = ((), (), s32[]{:S(2)}) async-start(), calls=%async_computation.13 | async-start | bytes 15204352 | tf_op jit(solution)/shard_map/psum | solution.py:329
  1930.6 217.5 %reduce-scatter.11.cloned.1.call-start = ((), (), s32[]{:S(2)}) async-start(), calls=%async_computation.10 | async-start | bytes 6291456 | tf_op jit(solution)/shard_map/reduce_scatter | solution.py:78
  1973.7 365.4 %all-gather.13.cloned.1.call-start = ((), (), s32[]{:S(2)}) async-start(), calls=%async_computation.11 | async-start | bytes 40108032 | tf_op jit(solution)/shard_map/all_gather | solution.py:17
  2103.0 51.0 %copy-start.96 = (bf16[256]{0:T(256)(128)(2,1)S(1)}, bf16[256]{0:T(256)(128)(2,1)}, u32[]{:S(2)}) copy-start(bf16[256]{0:T(256)(128)(2,1)} %get-tuple-element.270) | copy-start | bytes 1540
  2103.0 51.0 %copy-start.98 = (bf16[256]{0:T(256)(128)(2,1)S(1)}, bf16[256]{0:T(256)(128)(2,1)}, u32[]{:S(2)}) copy-start(bf16[256]{0:T(256)(128)(2,1)} %get-tuple-element.337) | copy-start | bytes 1540
  2103.0 51.0 %copy-start.99 = (bf16[256]{0:T(256)(128)(2,1)S(1)}, bf16[256]{0:T(256)(128)(2,1)}, u32[]{:S(2)}) copy-start(bf16[256]{0:T(256)(128)(2,1)} %get-tuple-element.370) | copy-start | bytes 1540
  2103.0 94.1 %copy-start.102 = (f32[16]{0:T(128)S(1)}, f32[16]{0:T(128)}, u32[]{:S(2)}) copy-start(f32[16]{0:T(128)} %copy-done.101) | copy-start | bytes 196
  2103.0 95.4 %copy-start.60 = (f32[256]{0:T(256)S(1)}, f32[256]{0:T(256)}, u32[]{:S(2)}) copy-start(f32[256]{0:T(256)} %copy-done.58) | copy-start | bytes 3076
  2103.0 95.4 %copy-start.73 = (f32[256]{0:T(256)S(1)}, f32[256]{0:T(256)}, u32[]{:S(2)}) copy-start(f32[256]{0:T(256)} %copy-done.71) | copy-start | bytes 3076
  2103.0 95.4 %copy-start.79 = (f32[256]{0:T(256)S(1)}, f32[256]{0:T(256)}, u32[]{:S(2)}) copy-start(f32[256]{0:T(256)} %copy-done.78) | copy-start | bytes 3076
  2103.0 95.4 %copy-start.82 = (f32[256]{0:T(256)S(1)}, f32[256]{0:T(256)}, u32[]{:S(2)}) copy-start(f32[256]{0:T(256)} %param.42) | copy-start | bytes 3076
  2103.0 95.4 %copy-start.88 = (f32[256]{0:T(256)S(1)}, f32[256]{0:T(256)}, u32[]{:S(2)}) copy-start(f32[256]{0:T(256)} %copy-done.87) | copy-start | bytes 3076
  (111 other events, 1315.6 us)
Sparse Core Ops, SparseCore 0:
  21.7 59.4 all-gather.6
  150.2 56.7 all-gather.14
  209.3 54.2 reduce-scatter.4
  265.0 56.7 all-gather.8
  1686.5 54.2 reduce-scatter.6
  1742.7 56.7 all-gather.10
  1825.9 54.4 reduce-scatter.8
  1930.7 160.2 all-reduce.9
  2093.9 54.1 reduce-scatter.10
  2149.6 189.4 all-gather.12
